TPU v7x, 128 devices: a whole 4x4x4 slice. The times are simulated.
128 devices in a mesh: tm: 64 (over x, z, y), head: 2 (over core).
Axes of the slice: x: 4, y: 4, z: 4, core: 2. Of those that a mesh axis runs over, the one named last changes fastest.
Arguments:
- series: bfloat16 [16, 65536, 512], P(None, 'tm'), may hold values from -6 to 6
- modes: int32 [128], replicated, may hold values from 1 to 32767, as said below
- query_weight: bfloat16 [512, 512], P(None, 'head'), may hold values from -0.25 to 0.25
- mix_weight: float32 [128, 8, 64, 128], P('tm', 'head'), may hold values from -0.5 to 0.5
- out_weight: bfloat16 [512, 512], P(None, 'head'), may hold values from -0.25 to 0.25
Outputs:
- output: bfloat16 [16, 65536, 512], P(None, 'tm', 'head')
Inputs may be any that keep to these rules, and one draw needn't show every extreme that they name: `modes`: distinct mode numbers; both 1 and one less than half of 65536 are among them.
All inputs are finite; a program needn't handle non-finite values.
Results may differ from a plain program's by a relative error of at most 0.0075.
Values may be sent and summed in bfloat16 or wider, within the bound.
A program may use at most 128 MiB of HBM per device.

v0:
```python
import math
import jax
import jax.numpy as jnp
from jax import lax
from jax.sharding import PartitionSpec as P

two_pi = 2.0 * math.pi


def wave_tables(mode_list, first_time, time_count, series_length):
    time_index = first_time + lax.iota(jnp.int32, time_count)
    phases = time_index[:, None] * mode_list[None, :] % series_length
    angles = phases.astype(jnp.float32) * (two_pi / series_length)
    return (jnp.cos(angles).astype(jnp.bfloat16), jnp.sin(angles).astype(jnp.bfloat16))


def body(series, modes, query_weight, mix_weight, out_weight):
    series_count, shard_rows, model_width = series.shape
    group_width = query_weight.shape[1]
    mode_total = modes.shape[0]
    own_modes = mix_weight.shape[0]
    heads_here = mix_weight.shape[1]
    head_size = mix_weight.shape[2]
    series_length = lax.axis_size("tm") * shard_rows
    first_time = lax.axis_index("tm") * shard_rows
    forward_scale = 1.0 / math.sqrt(series_length)
    inverse_scale = 1.0 / math.sqrt(mode_total)
    queries = jnp.dot(
        series.reshape(series_count * shard_rows, model_width),
        query_weight,
        preferred_element_type=jnp.float32,
    )
    queries = queries.astype(jnp.bfloat16).reshape(series_count, shard_rows, group_width)
    cosine, sine_part = wave_tables(modes, first_time, shard_rows, series_length)
    real_part = jnp.einsum("tm,btf->mbf", cosine, queries, preferred_element_type=jnp.float32)
    imag_part = jnp.einsum("tm,btf->mbf", sine_part, queries, preferred_element_type=jnp.float32)
    summed_all = lax.psum(jnp.stack([real_part, -imag_part], axis=1) * forward_scale, "tm")
    spectrum = lax.dynamic_slice_in_dim(summed_all, lax.axis_index("tm") * own_modes, own_modes, 0)
    spec_parts = spectrum.reshape(own_modes, 2, series_count, heads_here, head_size)
    from_real = jnp.einsum(
        "mbhi,mhio->mbho", spec_parts[:, 0], mix_weight, precision=lax.Precision.HIGHEST
    )
    from_imag = jnp.einsum(
        "mbhi,mhio->mbho", spec_parts[:, 1], mix_weight, precision=lax.Precision.HIGHEST
    )
    mixed_real = from_real[..., :head_size] - from_imag[..., head_size:]
    mixed_imag = from_real[..., head_size:] + from_imag[..., :head_size]
    mixed_spectra = jnp.stack([mixed_real, mixed_imag], axis=1).reshape(
        own_modes, 2, series_count, group_width
    )
    mixed_spectra = mixed_spectra.astype(jnp.bfloat16)
    cosine, sine_part = wave_tables(modes, first_time, shard_rows, series_length)
    wave_table = jnp.concatenate([cosine, -sine_part], axis=1)
    by_mode = lax.all_gather(mixed_spectra, "tm", axis=0, tiled=True)
    all_spectra = lax.all_gather(by_mode, "head", axis=3, tiled=True)
    stacked = jnp.concatenate([all_spectra[:, 0], all_spectra[:, 1]], axis=0)
    summed = jnp.einsum("tk,kbf->btf", wave_table, stacked, preferred_element_type=jnp.float32)
    restored = (summed * inverse_scale).astype(jnp.bfloat16)
    output = jnp.dot(
        restored.reshape(series_count * shard_rows, model_width),
        out_weight,
        preferred_element_type=jnp.float32,
    )
    return output.astype(jnp.bfloat16).reshape(series_count, shard_rows, group_width)


def solution(mesh):
    in_specs = (
        P(None, "tm", None),
        P(),
        P(None, "head"),
        P("tm", "head", None, None),
        P(None, "head"),
    )
    out_specs = P(None, "tm", "head")
    return jax.shard_map(body, mesh=mesh, in_specs=in_specs, out_specs=out_specs, check_vma=False)
```

profile of v0, /device:TPU:1, one launch (start us, length us, event | category | flops | bytes accessed | tf_op | source)
XLA Modules:
  0.0 306.4 jit_solution(206311727932910354)
XLA Ops:
  6.5 0.0 copy-start
  6.5 0.0 all-reduce.2.cloned.1.call-start
  6.5 0.9 copy-done
  7.5 0.0 copy-start.3
  7.5 10.3 %convolution_convert_fusion.1 = bf16[16384,256]{1,0:T(8,128)(2,1)S(1)} fusion(bf16[16384,512]{1,0:T(8,128)(2,1)} %bitcast.50, bf16[512,256]{1,0:T(8,128)(2,1)S(1)} %copy-done), kind=kOutput, calls=%fused_computation.2 | convolution fusion | flops 4299161600 | bytes 25427968 | tf_op jit(solution)/shard_map/dot_general | solution.py:28
  17.8 0.0 copy-done.3
  17.8 3.0 negate_bitcast_fusion
  20.8 3.0 convolution_bitcast_fusion
  23.8 2.4 maximum_multiply_fusion
  26.2 0.0 copy-start.2
  26.2 0.0 all-reduce.2.cloned.1.call-update
  26.3 0.0 all-gather.3.cloned.1.call-start
  26.3 140.7 %all-reduce.2.cloned.1.call-done = f32[128,2,16,256]{3,0,2,1:T(8,128)} async-done(((f32[128,2,16,256]{3,0,2,1:T(8,128)}), f32[128,2,16,256]{3,0,2,1:T(8,128)}) %all-reduce.2.cloned.1.call-update) | async-done | bytes 4194320 | tf_op jit(solution)/shard_map/psum | solution.py:37
  167.0 1.0 constant_dynamic-slice_fusion
  168.0 0.1 reshape.35
  168.1 0.0 copy-done.2
  168.1 0.3 convolution_bitcast_fusion.2
  168.5 0.3 convolution_bitcast_fusion.1
  168.8 0.1 fusion.13
  168.9 0.1 stack.21
  169.1 0.1 stack.22
  169.2 0.6 pad_maximum_fusion
  169.8 0.0 all-gather.3.cloned.1.call-update
  169.8 0.2 all-gather.5.cloned.1.call-start
  170.0 63.9 %all-gather.3.cloned.1.call-done = bf16[128,2,16,256]{3,2,1,0:T(8,128)(2,1)} async-done(((bf16[2,2,16,256]{3,2,1,0:T(8,128)(2,1)}), bf16[128,2,16,256]{3,2,1,0:T(8,128)(2,1)}) %all-gather.3.cloned.1.call-update) | async-done | bytes 2097168 | tf_op jit(solution)/shard_map/all_gather | solution.py:54
  233.9 4.5 %copy.27 = bf16[128,2,16,256]{0,3,2,1:T(8,128)(2,1)} copy(bf16[128,2,16,256]{3,2,1,0:T(8,128)(2,1)} %all-gather.3.cloned.1.call-done) | data formatting | bytes 4194304 | tf_op jit(solution)/shard_map/all_gather | solution.py:54
  238.4 0.0 all-gather.5.cloned.1.call-update
  238.4 2.3 fusion.11
  240.7 2.3 cosine_convert_fusion
  243.0 10.8 %all-gather.5.cloned.1.call-done = bf16[128,2,16,512]{0,3,2,1:T(8,128)(2,1)} async-done(((bf16[128,2,16,256]{0,3,2,1:T(8,128)(2,1)}), bf16[128,2,16,512]{0,3,2,1:T(8,128)(2,1)}) %all-gather.5.cloned.1.call-update) | async-done | bytes 4194320 | tf_op jit(solution)/shard_map/all_gather | solution.py:55
  253.8 2.5 slice_bitcast_fusion.1
  256.4 8.2 %fusion = bf16[16,1024,512]{1,2,0:T(8,128)(2,1)} fusion(bf16[128,16,512]{0,2,1:T(8,128)(2,1)S(1)} %get-tuple-element.6, bf16[128,16,512]{0,2,1:T(8,128)(2,1)S(1)} %get-tuple-element.5, bf16[1024,128]{1,0:T(8,128)(2,1)S(1)} %fusion.11, bf16[1024,128]{1,0:T(8,128)(2,1)S(1)} %cosine_convert_fusion), kind=kOutput, calls=%fused_computation.3 | convolution fusion | flops 4321181696 | bytes 21495808 | tf_op jit(solution)/shard_map/tk,kbf->btf/dot_general | solution.py:57
  264.5 0.0 copy-start.4
  264.5 21.7 %copy.28 = bf16[16,1024,512]{2,1,0:T(8,128)(2,1)} copy(bf16[16,1024,512]{1,2,0:T(8,128)(2,1)} %fusion) | data formatting | bytes 33554432 | tf_op jit(solution)/shard_map/convert_element_type | solution.py:58
  286.2 0.0 copy-done.4
  286.2 0.0 copy-start.1
  286.2 13.7 %convolution_convert_fusion = bf16[16384,256]{1,0:T(8,128)(2,1)} fusion(bf16[16384,512]{1,0:T(8,128)(2,1)} %bitcast.47, bf16[512,256]{1,0:T(8,128)(2,1)S(1)} %copy-done.4), kind=kOutput, calls=%fused_computation.1 | convolution fusion | flops 4299161600 | bytes 25427968 | tf_op jit(solution)/shard_map/dot_general | solution.py:59
  299.9 0.0 copy-done.1
  (4 shorter events, 0.0 us)
Async XLA Ops:
  6.5 1.0 copy-start
  6.5 160.4 %all-reduce.2.cloned.1.call-start = ((), (), s32[]{:S(2)}) async-start(), calls=%async_computation | async-start | bytes 8388608 | tf_op jit(solution)/shard_map/psum | solution.py:37
  7.5 10.3 %copy-start.3 = (s32[128]{0:T(128)S(1)}, s32[128]{0:T(128)}, u32[]{:S(2)}) copy-start(s32[128]{0:T(128)} %param.6) | copy-start | bytes 1540
  26.2 141.9 %copy-start.2 = (f32[2,4,64,128]{3,2,1,0:T(8,128)S(1)}, f32[2,4,64,128]{3,2,1,0:T(8,128)}, u32[]{:S(2)}) copy-start(f32[2,4,64,128]{3,2,1,0:T(8,128)} %param.8) | copy-start | bytes 786436
  26.3 207.6 %all-gather.3.cloned.1.call-start = ((), (), s32[]{:S(2)}) async-start(), calls=%async_computation.1 | async-start | bytes 2129920 | tf_op jit(solution)/shard_map/all_gather | solution.py:54
  169.8 84.0 %all-gather.5.cloned.1.call-start = ((), (), s32[]{:S(2)}) async-start(), calls=%async_computation.2 | async-start | bytes 6291456 | tf_op jit(solution)/shard_map/all_gather | solution.py:55
  264.5 21.7 %copy-start.4 = (bf16[512,256]{1,0:T(8,128)(2,1)S(1)}, bf16[512,256]{1,0:T(8,128)(2,1)}, u32[]{:S(2)}) copy-start(bf16[512,256]{1,0:T(8,128)(2,1)} %param.9) | copy-start | bytes 786436
  286.2 13.7 %copy-start.1 = (bf16[512,256]{1,0:T(8,128)(2,1)S(1)}, bf16[512,256]{1,0:T(8,128)(2,1)}, u32[]{:S(2)}) copy-start(bf16[512,256]{1,0:T(8,128)(2,1)} %param.7) | copy-start | bytes 786436
Sparse Core Ops, SparseCore 0:
  26.4 140.5 all-reduce.1
  170.3 63.6 all-gather.2
  238.6 15.2 all-gather.4
where the time goes:
time: 307 us; the launch traced here: 306 us
  waiting for transfers between devices  215 us (70%)
  matrix products  38.9 us (13%)
  local copies, waits for them, and re-layouts  31 us (10%)
  between operations  13.2 us (4%)
  other arithmetic  7.68 us (3%)
    psum x1, waiting for transfers between devices, body(): lax.psum(jnp.stack([real_part, -imag_part], axis=1) * forward_scale, 'tm')  141 us
    all_gather x1, waiting for transfers between devices, body(): by_mode = lax.all_gather(mixed_spectra, 'tm', axis=0, tiled=True)  63.9 us
    convert_element_type x1, local copies, waits for them, and re-layouts, body(): restored = (summed * inverse_scale).astype(jnp.bfloat16)  21.7 us
    dot_general x1, matrix products, body(): jnp.dot(restored.reshape(series_count * shard_rows, model_width), out_wei...  13.7 us
    all_gather x1, waiting for transfers between devices, body(): all_spectra = lax.all_gather(by_mode, 'head', axis=3, tiled=True)  10.8 us
    dot_general x1, matrix products, body(): jnp.dot(series.reshape(series_count * shard_rows, model_width), query_wei...  10.3 us
    dot_general x1, matrix products, body(): jnp.einsum('tk,kbf->btf', wave_table, stacked, preferred_element_type=jnp...  8.16 us
  transfers between devices with their start and end apart: 3, of which 3 were waited for; matrix products, arithmetic and copies ran while one was open for 1% of the time, Pallas kernels for 0%

commit v1 on v0

--- a/solution.py
+++ b/solution.py
@@ -5,6 +5,11 @@
 from jax.sharding import PartitionSpec as P
 
 two_pi = 2.0 * math.pi
+
+
+def gather_over(value, axis, d):
+    sent = jnp.stack([value] * lax.axis_size(axis))
+    return jnp.concatenate(lax.all_to_all(sent, axis, 0, 0), axis=d)
 
 
 def wave_tables(mode_list, first_time, time_count, series_length):
@@ -52,7 +57,7 @@
     cosine, sine_part = wave_tables(modes, first_time, shard_rows, series_length)
     wave_table = jnp.concatenate([cosine, -sine_part], axis=1)
     by_mode = lax.all_gather(mixed_spectra, "tm", axis=0, tiled=True)
-    all_spectra = lax.all_gather(by_mode, "head", axis=3, tiled=True)
+    all_spectra = gather_over(by_mode, "head", 3)
     stacked = jnp.concatenate([all_spectra[:, 0], all_spectra[:, 1]], axis=0)
     summed = jnp.einsum("tk,kbf->btf", wave_table, stacked, preferred_element_type=jnp.float32)
     restored = (summed * inverse_scale).astype(jnp.bfloat16)

time: 307 us -> 308 us (level)
  waiting for transfers between devices: 215 us -> 199 us
  blocking collectives: 0 us -> 10.2 us
  local copies, waits for them, and re-layouts: 31 us -> 34.3 us
    all_gather x1 -> x0, waiting for transfers between devices: 10.8 us -> none  [body(): all_spectra = lax.all_gather(by_mode, 'head', axis=3, tiled=True)]
    all_to_all x0 -> x1, blocking collectives: none -> 10.2 us  [gather_over(): return jnp.concatenate(lax.all_to_all(sent, axis, 0, 0), axis=d)]
    reshape x0 -> x1, local copies, waits for them, and re-layouts: none -> 7.86 us  [gather_over(): return jnp.concatenate(lax.all_to_all(sent, axis, 0, 0), axis=d)]
    all_gather x1, waiting for transfers between devices: 63.9 us -> 59 us  [body(): by_mode = lax.all_gather(mixed_spectra, 'tm', axis=0, tiled=True)]
    all_gather x1 -> x0, local copies, waits for them, and re-layouts: 4.51 us -> none  [body(): by_mode = lax.all_gather(mixed_spectra, 'tm', axis=0, tiled=True)]
  transfers between devices with their start and end apart: 3 -> 2, of which waited for: 3 -> 2; matrix products, arithmetic and copies ran while one was open for 1% -> 1% of each run, Pallas kernels for 0% -> 0%
where the time goes in v1:
time: 308 us; the launch traced here: 307 us
  waiting for transfers between devices  199 us (65%)
  matrix products  38.9 us (13%)
  local copies, waits for them, and re-layouts  34.3 us (11%)
  between operations  13.5 us (4%)
  other arithmetic  10.3 us (3%)
  blocking collectives  10.2 us (3%)
    psum x1, waiting for transfers between devices, body(): lax.psum(jnp.stack([real_part, -imag_part], axis=1) * forward_scale, 'tm')  140 us
    all_gather x1, waiting for transfers between devices, body(): by_mode = lax.all_gather(mixed_spectra, 'tm', axis=0, tiled=True)  59 us
    convert_element_type x1, local copies, waits for them, and re-layouts, body(): restored = (summed * inverse_scale).astype(jnp.bfloat16)  21.6 us
    dot_general x1, matrix products, body(): jnp.dot(restored.reshape(series_count * shard_rows, model_width), out_wei...  13.7 us
    dot_general x1, matrix products, body(): jnp.dot(series.reshape(series_count * shard_rows, model_width), query_wei...  10.3 us
    all_to_all x1, blocking collectives, gather_over(): return jnp.concatenate(lax.all_to_all(sent, axis, 0, 0), axis=d)  10.2 us
    dot_general x1, matrix products, body(): jnp.einsum('tk,kbf->btf', wave_table, stacked, preferred_element_type=jnp...  8.15 us
    reshape x1, local copies, waits for them, and re-layouts, gather_over(): return jnp.concatenate(lax.all_to_all(sent, axis, 0, 0), axis=d)  7.86 us
  transfers between devices with their start and end apart: 2, of which 2 were waited for; matrix products, arithmetic and copies ran while one was open for 1% of the time, Pallas kernels for 0%

profile of v1, /device:TPU:1, one launch (start us, length us, event | category | flops | bytes accessed | tf_op | source)
XLA Modules:
  0.0 306.8 jit_solution(12860841057305628679)
XLA Ops:
  6.5 0.0 copy-start
  6.5 0.0 all-reduce.2.cloned.1.call-start
  6.5 0.9 copy-done
  7.5 0.0 copy-start.3
  7.5 10.3 %convolution_convert_fusion.1 = bf16[16384,256]{1,0:T(8,128)(2,1)S(1)} fusion(bf16[16384,512]{1,0:T(8,128)(2,1)} %bitcast.52, bf16[512,256]{1,0:T(8,128)(2,1)S(1)} %copy-done), kind=kOutput, calls=%fused_computation.2 | convolution fusion | flops 4299161600 | bytes 25427968 | tf_op jit(solution)/shard_map/dot_general | solution.py:33
  17.8 0.0 copy-done.3
  17.8 3.0 negate_bitcast_fusion
  20.8 3.0 convolution_bitcast_fusion
  23.8 2.4 maximum_multiply_fusion
  26.2 0.0 copy-start.2
  26.2 0.0 all-reduce.2.cloned.1.call-update
  26.3 0.2 all-gather.2.cloned.1.call-start
  26.5 140.5 %all-reduce.2.cloned.1.call-done = f32[128,2,16,256]{3,0,2,1:T(8,128)} async-done(((f32[128,2,16,256]{3,0,2,1:T(8,128)}), f32[128,2,16,256]{3,0,2,1:T(8,128)}) %all-reduce.2.cloned.1.call-update) | async-done | bytes 4194320 | tf_op jit(solution)/shard_map/psum | solution.py:42
  167.0 1.0 constant_dynamic-slice_fusion
  168.0 0.1 reshape.43
  168.1 0.0 copy-done.2
  168.1 0.3 convolution_bitcast_fusion.2
  168.5 0.3 convolution_bitcast_fusion.1
  168.8 0.1 fusion.13
  168.9 0.1 stack.28
  169.1 0.1 stack.29
  169.2 0.6 pad_maximum_fusion.1
  169.8 0.0 all-gather.2.cloned.1.call-update
  169.8 2.3 fusion.11
  172.1 2.3 cosine_convert_fusion
  174.4 59.0 %all-gather.2.cloned.1.call-done = bf16[128,2,16,256]{3,2,0,1:T(8,128)(2,1)} async-done(((bf16[2,2,16,256]{3,2,0,1:T(8,128)(2,1)}), bf16[128,2,16,256]{3,2,0,1:T(8,128)(2,1)}) %all-gather.2.cloned.1.call-update) | async-done | bytes 2097168 | tf_op jit(solution)/shard_map/all_gather | solution.py:59
  233.3 2.6 pad_maximum_fusion
  236.0 10.2 %all_to_all.5 = bf16[2,128,2,16,256]{4,3,1,2,0:T(8,128)(2,1)} all-to-all(bf16[2,128,2,16,256]{4,3,1,2,0:T(8,128)(2,1)S(1)} %pad_maximum_fusion), channel_id=1, replica_groups=mesh['tm'=64,'head'=2] {'head'}, dimensions={0} | all-to-all | bytes 8388608 | tf_op jit(solution)/shard_map/all_to_all | solution.py:12
  246.1 7.9 %copy.15 = bf16[128,2,16,2,256]{0,4,3,2,1:T(8,128)(2,1)} copy(bf16[128,2,16,2,256]{4,2,0,1,3:T(8,128)(2,1)} %bitcast.50) | data formatting | bytes 8388608 | tf_op jit(solution)/shard_map/reshape | solution.py:12
  254.0 2.5 slice_bitcast_fusion.1
  256.5 8.1 %fusion = bf16[16,1024,512]{1,2,0:T(8,128)(2,1)} fusion(bf16[128,16,512]{0,2,1:T(8,128)(2,1)S(1)} %get-tuple-element.6, bf16[128,16,512]{0,2,1:T(8,128)(2,1)S(1)} %get-tuple-element.5, bf16[1024,128]{1,0:T(8,128)(2,1)S(1)} %fusion.11, bf16[1024,128]{1,0:T(8,128)(2,1)S(1)} %cosine_convert_fusion), kind=kOutput, calls=%fused_computation.3 | convolution fusion | flops 4321181696 | bytes 21495808 | tf_op jit(solution)/shard_map/tk,kbf->btf/dot_general | solution.py:62
  264.6 0.0 copy-start.4
  264.6 21.6 %copy.16 = bf16[16,1024,512]{2,1,0:T(8,128)(2,1)} copy(bf16[16,1024,512]{1,2,0:T(8,128)(2,1)} %fusion) | data formatting | bytes 33554432 | tf_op jit(solution)/shard_map/convert_element_type | solution.py:63
  286.3 0.0 copy-done.4
  286.3 0.0 copy-start.1
  286.3 13.7 %convolution_convert_fusion = bf16[16384,256]{1,0:T(8,128)(2,1)} fusion(bf16[16384,512]{1,0:T(8,128)(2,1)} %bitcast.48, bf16[512,256]{1,0:T(8,128)(2,1)S(1)} %copy-done.4), kind=kOutput, calls=%fused_computation.1 | convolution fusion | flops 4299161600 | bytes 25427968 | tf_op jit(solution)/shard_map/dot_general | solution.py:64
  300.0 0.0 copy-done.1
  (4 shorter events, 0.0 us)
Async XLA Ops:
  6.5 1.0 copy-start
  6.5 160.4 %all-reduce.2.cloned.1.call-start = ((), (), s32[]{:S(2)}) async-start(), calls=%async_computation.1 | async-start | bytes 8388608 | tf_op jit(solution)/shard_map/psum | solution.py:42
  7.5 10.3 %copy-start.3 = (s32[128]{0:T(128)S(1)}, s32[128]{0:T(128)}, u32[]{:S(2)}) copy-start(s32[128]{0:T(128)} %param.6) | copy-start | bytes 1540
  26.2 141.9 %copy-start.2 = (f32[2,4,64,128]{3,2,1,0:T(8,128)S(1)}, f32[2,4,64,128]{3,2,1,0:T(8,128)}, u32[]{:S(2)}) copy-start(f32[2,4,64,128]{3,2,1,0:T(8,128)} %param.8) | copy-start | bytes 786436
  26.3 207.1 %all-gather.2.cloned.1.call-start = ((), (), s32[]{:S(2)}) async-start(), calls=%async_computation.2 | async-start | bytes 2129920 | tf_op jit(solution)/shard_map/all_gather | solution.py:59
  264.6 21.6 %copy-start.4 = (bf16[512,256]{1,0:T(8,128)(2,1)S(1)}, bf16[512,256]{1,0:T(8,128)(2,1)}, u32[]{:S(2)}) copy-start(bf16[512,256]{1,0:T(8,128)(2,1)} %param.9) | copy-start | bytes 786436
  286.3 13.7 %copy-start.1 = (bf16[512,256]{1,0:T(8,128)(2,1)S(1)}, bf16[512,256]{1,0:T(8,128)(2,1)}, u32[]{:S(2)}) copy-start(bf16[512,256]{1,0:T(8,128)(2,1)} %param.7) | copy-start | bytes 786436
Sparse Core Ops, SparseCore 0:
  26.4 140.5 all-reduce.1
  170.3 62.9 all-gather.1
